TPU v7x, 512 devices: a whole 4x8x8 slice. The times are simulated.
512 devices in a mesh: day: 32 (over z, y_hi), sta: 16 (over y_lo, x, core).
Axes of the slice: x: 4, y: 8 (y_hi: 4, y_lo: 2; y = y_hi * 2 + y_lo), z: 8, core: 2. Of those that a mesh axis runs over, the one named last changes fastest.
Arguments:
- spectra: bfloat16 [2048, 2, 3, 384, 128], P('day', None, None, 'sta'), may hold values from -6 to 6
- src_block: int32 [2], replicated, may hold values from 0 to 15, as said below
- group_of: int32 [2048], replicated, may hold values from 0 to 1, as said below
- owner: int32 [32], replicated, may hold values from 0 to 31, each once
Outputs:
- owned_stacks: float32 [32, 96, 2, 9, 128], P('day', 'sta')
Inputs may be any that keep to these rules, and one draw needn't show every extreme that they name: `src_block`: the two entries differ. `group_of`: every one of the 2 groups has at least one segment. `owner`: each day index owns exactly one pair block.
All inputs are finite; a program needn't handle non-finite values.
Results may differ from a plain program's by a relative error of at most 0.0003.
Values may be sent and summed in bfloat16 or wider, within the bound.
A program may use at most 64 MiB of HBM per device.

v0:
```python
import jax
import jax.numpy as jnp
from jax import lax
from jax.sharding import PartitionSpec as P

F = 128
LAG = 128
G = 2
SB = 4
S = 8


def from_root(value, axis, source):
    kept = jnp.where(lax.axis_index(axis) == source, value, 0).astype(value.dtype)
    return lax.psum(kept, axis)


def lag_table(freqs, lags):
    freq_ids = jnp.arange(freqs, dtype=jnp.int32)
    lag_ids = jnp.arange(lags, dtype=jnp.int32) - lags // 2
    phase = jnp.mod(freq_ids[:, None] * lag_ids[None, :], 2 * freqs)
    angle = 2.0 * jnp.pi / (2 * freqs) * phase.astype(jnp.float32)
    weight = jnp.where(freq_ids == 0, 1.0, 2.0).astype(jnp.float32) / jnp.sqrt(jnp.float32(freqs))
    return jnp.concatenate(
        [weight[:, None] * jnp.cos(angle), -weight[:, None] * jnp.sin(angle)], axis=0
    )


def cross_terms(onehot, sources, spectra, scale_rows):
    weighted = onehot[:, :, None, None, None, None] * sources[None]
    real_part = jnp.einsum(
        "gtpasf,tpbrf->srgabf", weighted, spectra, preferred_element_type=jnp.float32
    )
    swapped = jnp.stack([spectra[:, 1], -spectra[:, 0]], axis=1)
    imag_part = jnp.einsum(
        "gtpasf,tpbrf->srgabf", weighted, swapped, preferred_element_type=jnp.float32
    )
    scaled = scale_rows[None, None, :, None, None, None]
    return (real_part * scaled, imag_part * scaled)


def owner_order(blocks, owner, day_count):
    day_ids = jnp.arange(day_count, dtype=jnp.int32)
    inverse = jnp.sum(
        day_ids[None, :] * (owner[None, :] == day_ids[:, None]).astype(jnp.int32), axis=1
    )
    return jnp.take(blocks, inverse, axis=0)


def local(spectra, src_block, group_of, owner):
    seg_count = spectra.shape[0]
    receivers = spectra.shape[3]
    day_count = lax.axis_size("day")
    day_index = lax.axis_index("day")
    group_ids = jnp.arange(G, dtype=jnp.int32)
    all_hot = (group_of[None, :] == group_ids[:, None]).astype(jnp.float32)
    counts = jnp.sum(all_hot, axis=1)
    scale_rows = 1.0 / jnp.sqrt(counts)
    pair_count = S * receivers
    block_rows = pair_count // day_count
    table = lag_table(F, LAG)
    my_groups = lax.dynamic_slice_in_dim(group_of, day_index * seg_count, seg_count)
    onehot = (my_groups[None, :] == group_ids[:, None]).astype(jnp.bfloat16)
    first_rows = spectra[:, :, :, :SB, :]
    gathered = []
    for block_number in range(2):
        gathered.append(from_root(first_rows, "sta", src_block[block_number]))
    sources = jnp.concatenate(gathered, axis=3)
    real_part, imag_part = cross_terms(onehot, sources, spectra, scale_rows)
    spectra_pairs = jnp.concatenate([real_part, imag_part], axis=-1)
    blocks = spectra_pairs.reshape(day_count, block_rows, G, 9, 2 * F)
    ordered = owner_order(blocks, owner, day_count).reshape(day_count * block_rows, G, 9, 2 * F)
    result = jnp.dot(ordered.reshape(-1, 2 * F), table, precision=lax.Precision.HIGHEST)
    mine = lax.psum_scatter(
        result.reshape(block_rows * lax.axis_size("day"), G, 9, LAG),
        "day",
        scatter_dimension=0,
        tiled=True,
    )
    return mine.reshape(1, block_rows, G, 9, LAG)


def solution(mesh):
    return jax.shard_map(
        local,
        mesh=mesh,
        in_specs=(P("day", None, None, "sta", None), P(), P(), P()),
        out_specs=P("day", "sta", None, None, None),
        check_vma=False,
    )
```

profile of v0, /device:TPU:6, one launch (start us, length us, event | category | flops | bytes accessed | tf_op | source)
XLA Modules:
  0.0 546.0 jit_solution(13817798452652893278)
XLA Ops:
  6.5 0.0 all-reduce.7.cloned.1.call-start
  6.5 1.4 fusion.25
  9.3 0.0 copy-start.2
  9.3 2.3 broadcast_select_fusion.1
  11.6 0.0 all-reduce.7.cloned.1.call-update
  11.6 0.0 all-reduce.5.cloned.1.call-start
  11.6 2.1 fusion.24
  13.7 0.0 copy-done.2
  13.7 0.1 fusion.18
  13.9 0.6 dynamic_slice.3
  14.5 2.8 copy.64
  17.3 0.0 copy-start
  17.3 3.7 neg.12
  21.0 2.8 copy.63
  23.8 0.0 copy-done
  23.8 0.0 copy-start.3
  23.8 0.0 copy-start.4
  23.8 4.8 copy.55
  28.6 0.0 copy-done.3
  28.7 0.1 select_reduce_fusion
  28.8 0.1 broadcast_in_dim.41
  28.9 0.1 broadcast_in_dim.42
  29.0 0.0 copy-done.4
  29.0 0.3 cosine_multiply_fusion
  29.3 113.3 %all-reduce.7.cloned.1.call-done = (bf16[64,2,3,4,128]{4,3,2,1,0:T(4,128)(2,1)}, bf16[64,2,3,4,128]{4,3,2,1,0:T(4,128)(2,1)}) async-done(((bf16[64,2,3,4,128]{4,3,2,1,0:T(4,128)(2,1)}, bf16[64,2,3,4,128]{4,3,2,1,0:T(4,128)(2,1)}), (bf16[64,2,3,4,128]{4,3,2,1,0:T(4,128)(2,1)}, bf16[64,2,3,4,128]{4,3,2,1,0:T(4,128)(2,1)})) %all-reduce.7.cloned.1.call-update) | async-done | bytes 786448 | tf_op jit(solution)/shard_map/psum | solution.py:15
  142.6 1.5 pad_maximum_fusion.1
  144.1 1.2 copy.43
  145.3 9.6 %fusion.5 = f32[128,3,24,2,3,8]{2,5,4,3,1,0:T(8,128)} fusion(bf16[64,1,3,24,128]{0,3,1,2,4:T(8,128)(2,1)} %neg.12, bf16[64,1,3,24,128]{0,3,1,2,4:T(8,128)(2,1)} %copy.63, bf16[64,2,3,8,128]{0,3,1,2,4:T(8,128)(2,1)S(1)} %copy.43, bf16[2,64]{1,0:T(2,128)(2,1)S(1)} %compare_convert_fusion.1), kind=kOutput, calls=%fused_computation.11 | convolution fusion | flops 121110528 | bytes 4915456 | tf_op jit(solution)/shard_map/gtpasf,tpbrf->srgabf/dot_general | solution.py:35
  155.0 6.4 %copy.48 = f32[128,3,24,2,3,8]{0,5,4,3,2,1:T(8,128)S(1)} copy(f32[128,3,24,2,3,8]{2,5,4,3,1,0:T(8,128)} %fusion.5) | data formatting | bytes 3538944 | tf_op jit(solution)/shard_map/gtpasf,tpbrf->srgabf/dot_general | solution.py:35
  161.4 11.9 %convolution_bitcast_fusion = f32[128,2,3,8,3,24]{5,3,4,2,1,0:T(8,128)} fusion(bf16[64,2,3,24,128,1,1]{0,3,1,2,6,5,4:T(8,128)(2,1)} %copy.55, bf16[64,2,3,8,128]{0,3,1,2,4:T(8,128)(2,1)S(1)} %copy.43, bf16[2,64]{1,0:T(2,128)(2,1)S(1)} %compare_convert_fusion.1), kind=kOutput, calls=%fused_computation.12 | convolution fusion | flops 116391936 | bytes 4915456 | tf_op jit(solution)/shard_map/gtpasf,tpbrf->srgabf/dot_general | solution.py:31
  173.3 7.5 %copy.45 = f32[128,2,3,8,3,24]{0,3,2,1,5,4:T(8,128)} copy(f32[128,2,3,8,3,24]{5,3,4,2,1,0:T(8,128)} %convolution_bitcast_fusion) | data formatting | bytes 3538944 | tf_op jit(solution)/shard_map/gtpasf,tpbrf->srgabf/dot_general | solution.py:31
  180.8 0.0 copy-start.1
  180.8 0.2 multiply_bitcast_fusion.4
  181.0 1.3 copy-done.1
  182.3 0.2 multiply_bitcast_fusion.5
  182.5 0.3 pad_maximum_fusion
  182.8 1.8 copy.49
  184.6 3.6 copy.50
  188.2 6.4 %gather_fusion = f32[32,6,2,9,256]{4,3,2,1,0:T(8,128)} fusion(f32[32,6,2,9,256]{4,3,2,1,0:T(8,128)} %copy.50, s32[1024]{0:T(1024)S(1)} %pad_clamp_fusion), kind=kCustom, calls=%fused_computation | custom fusion | bytes 7078016 | tf_op jit(solution)/shard_map/jit(_take)/gather | solution.py:47
  194.6 6.3 %copy.51 = f32[32,6,2,9,256]{4,2,3,1,0:T(2,128)S(1)} copy(f32[32,6,2,9,256]{4,3,2,1,0:T(8,128)} %gather_fusion) | data formatting | bytes 7077888 | tf_op jit(solution)/shard_map/jit(_take)/gather | solution.py:47
  200.9 1.8 bitcast_select_fusion
  202.7 3.0 fusion.3
  205.7 2.6 copy.53
  208.3 0.0 all-reduce.5.cloned.1.call-update
  208.3 1.3 dynamic-slice
  210.2 327.5 %all-reduce.5.cloned.1.call-done = f32[192,2,9,128]{3,1,2,0:T(2,128)} async-done(((f32[192,2,9,128]{3,1,2,0:T(2,128)}), f32[192,2,9,128]{3,1,2,0:T(2,128)}) %all-reduce.5.cloned.1.call-update) | async-done | bytes 1769488
  537.7 1.4 dynamic-slice_bitcast_fusion
  (7 shorter events, 0.0 us)
Async XLA Ops:
  6.5 136.0 %all-reduce.7.cloned.1.call-start = ((), (), s32[]{:S(2)}) async-start(), calls=%async_computation.1 | async-start | bytes 1572864 | tf_op jit(solution)/shard_map/psum | solution.py:15
  9.3 4.5 copy-start.2
  11.6 526.1 %all-reduce.5.cloned.1.call-start = ((), (), s32[]{:S(2)}) async-start(), calls=%async_computation | async-start | bytes 3538944
  17.3 6.5 %copy-start = (bf16[64,2,3,24,128]{4,3,2,1,0:T(8,128)(2,1)S(1)}, bf16[64,2,3,24,128]{4,3,2,1,0:T(8,128)(2,1)}, u32[]{:S(2)}) copy-start(bf16[64,2,3,24,128]{4,3,2,1,0:T(8,128)(2,1)} %param.4) | copy-start | bytes 7077892
  23.8 4.8 copy-start.3
  23.8 5.2 copy-start.4
  180.8 1.5 copy-start.1
Sparse Core Ops, SparseCore 0:
  11.7 130.8 all-reduce.6
  208.4 329.2 all-reduce.4
where the time goes:
time: 547 us; the launch traced here: 546 us
  waiting for transfers between devices  441 us (81%)
  local copies, waits for them, and re-layouts  54.4 us (10%)
  matrix products  24.6 us (4%)
  between operations  15.6 us (3%)
  other arithmetic  10.6 us (2%)
    unnamed x3, waiting for transfers between devices  328 us
    psum x1, waiting for transfers between devices, from_root(): return lax.psum(kept, axis)  113 us
    unnamed x14, local copies, waits for them, and re-layouts  13 us
    gather x2, local copies, waits for them, and re-layouts, owner_order(): return jnp.take(blocks, inverse, axis=0)  12.7 us
    dot_general x1, matrix products, cross_terms(): jnp.einsum('gtpasf,tpbrf->srgabf', weighted, spectra, preferred_element_t...  11.9 us
  transfers between devices with their start and end apart: 2, of which 2 were waited for; matrix products, arithmetic and copies ran while one was open for 3% of the time, Pallas kernels for 0%

commit v1 on v0

v1 whole, which is shorter than its diff:
```python
import jax
import jax.numpy as jnp
import numpy as np
from jax import lax
from jax.experimental import pallas as pl
from jax.experimental.pallas import tpu as pltpu
from jax.sharding import PartitionSpec as P

F = 128
LAG = 128
G = 2
SB = 4
S = 8
PB = 6
SEG = 64
R = 24
N_STA = 16
N_DAY = 32
N_Z = 8
N_Y = 4
PIECE = SEG // N_STA
ROWS = 112
UNROLL = 4
MESH = pl.DeviceIdType.MESH
VMEM_LIMIT = 48 * 1024 * 1024


def lag_tables():
    freq = np.arange(F)
    lag = np.arange(LAG) - LAG // 2
    angle = 2.0 * np.pi / (2 * F) * np.mod(freq[:, None] * lag[None, :], 2 * F)
    weight = np.where(freq == 0, 1.0, 2.0) / np.sqrt(F)
    table = np.concatenate(
        [weight[:, None] * np.cos(angle), -weight[:, None] * np.sin(angle)], axis=0
    )
    high = table.astype(jnp.bfloat16)
    low = (table - high.astype(np.float64)).astype(jnp.bfloat16)
    return high, low


def share_kernel(
    src_ref, spec_ref, out_ref, tiles, mine, seen, in_sem, a_send, a_recv, b_send, b_recv, c_send, c_recv
):
    me = lax.axis_index("sta")
    partner = me + 1 - 2 * lax.rem(me, 2)
    fetch = pltpu.make_async_copy(spec_ref.at[:, :, :, :, pl.ds(0, 8), :], tiles, in_sem)
    fetch.start()
    barrier = pltpu.get_barrier_semaphore()
    for step in range(1, N_STA):
        pl.semaphore_signal(
            barrier, inc=1, device_id={"sta": lax.rem(me + step, N_STA)}, device_id_type=MESH
        )
    pl.semaphore_wait(barrier, N_STA - 1)
    fetch.wait()
    for part in range(2):
        for comp in range(3):
            row = (part * 3 + comp) * SB
            mine[:, :, row : row + SB, :] = tiles[:, :, part, comp, 0:SB, :]

    def scatter(step):
        to = lax.rem(me + step, N_STA)
        return pltpu.make_async_remote_copy(
            src_ref=mine.at[to],
            dst_ref=seen.at[me],
            send_sem=a_send.at[step - 1],
            recv_sem=a_recv.at[step - 1],
            device_id={"sta": to},
            device_id_type=MESH,
        )

    scatters = [scatter(step) for step in range(1, N_STA)]
    for copy in scatters:
        copy.start()
    seen[me] = mine[me]
    for copy in scatters:
        copy.wait_recv()
    for block in range(2):
        out_ref[me, block] = seen[src_ref[block]]

    def spread(step):
        to = lax.rem(me + 2 * step, N_STA)
        return pltpu.make_async_remote_copy(
            src_ref=out_ref.at[me],
            dst_ref=out_ref.at[me],
            send_sem=b_send.at[step - 1],
            recv_sem=b_recv.at[step - 1],
            device_id={"sta": to},
            device_id_type=MESH,
        )

    def hand_over(step):
        piece = lax.rem(me + N_STA - 2 * step, N_STA)
        return pltpu.make_async_remote_copy(
            src_ref=out_ref.at[piece],
            dst_ref=out_ref.at[piece],
            send_sem=c_send.at[step],
            recv_sem=c_recv.at[step],
            device_id={"sta": partner},
            device_id_type=MESH,
        )

    half = N_STA // 2
    spreads = [spread(step) for step in range(1, half)]
    hands = [hand_over(step) for step in range(half)]
    for copy in spreads:
        copy.start()
    hands[0].start()
    for step in range(1, half):
        spreads[step - 1].wait_recv()
        hands[step].start()
    for copy in hands:
        copy.wait_recv()
    for copy in scatters + spreads + hands:
        copy.wait_send()


def share(src_block, spectra):
    pieces = spectra.reshape(N_STA, PIECE, 2, 3, R, F)
    half = N_STA // 2
    return pl.pallas_call(
        share_kernel,
        out_shape=jax.ShapeDtypeStruct((N_STA, 2, PIECE, 6 * SB, F), jnp.bfloat16),
        in_specs=[
            pl.BlockSpec(memory_space=pltpu.SMEM),
            pl.BlockSpec(memory_space=pl.ANY),
        ],
        out_specs=pl.BlockSpec(memory_space=pltpu.VMEM),
        scratch_shapes=[
            pltpu.VMEM((N_STA, PIECE, 2, 3, 8, F), jnp.bfloat16),
            pltpu.VMEM((N_STA, PIECE, 6 * SB, F), jnp.bfloat16),
            pltpu.VMEM((N_STA, PIECE, 6 * SB, F), jnp.bfloat16),
            pltpu.SemaphoreType.DMA,
            pltpu.SemaphoreType.DMA((N_STA - 1,)),
            pltpu.SemaphoreType.DMA((N_STA - 1,)),
            pltpu.SemaphoreType.DMA((half - 1,)),
            pltpu.SemaphoreType.DMA((half - 1,)),
            pltpu.SemaphoreType.DMA((half,)),
            pltpu.SemaphoreType.DMA((half,)),
        ],
        compiler_params=pltpu.CompilerParams(
            collective_id=0, has_side_effects=True, vmem_limit_bytes=VMEM_LIMIT
        ),
        name="share",
    )(src_block, pieces)


def stack_kernel(
    day_ref, group_ref, owner_ref, group_tile_ref, spec_ref, source_ref, high_ref, low_ref,
    out_ref, rec_re, rec_im, rec_sum, src_re, src_im, src_dif, cross, lagged, order,
):
    first = day_ref[0] * SEG

    def clear(i, carry):
        order[0, i] = SEG
        order[1, i] = SEG
        return carry

    lax.fori_loop(0, SEG + UNROLL, clear, 0)

    def sort(t, carry):
        zeros, ones = carry
        group = group_ref[first + t]
        order[group, jnp.where(group == 0, zeros, ones)] = t
        return zeros + 1 - group, ones + group

    zeros, ones = lax.fori_loop(0, SEG, sort, (jnp.int32(0), jnp.int32(0)))

    def widen(t, carry):
        for comp in range(3):
            real = spec_ref[t, 0, comp].astype(jnp.float32)
            imag = spec_ref[t, 1, comp].astype(jnp.float32)
            rec_re[t, comp] = real
            rec_im[t, comp] = imag
            rec_sum[t, comp] = real + imag
        for block in range(2):
            rows = source_ref[t // PIECE, block, lax.rem(t, PIECE)].astype(jnp.float32)
            real, imag = rows[: 3 * SB], rows[3 * SB :]
            at = pl.ds(block * 3 * SB, 3 * SB)
            src_re[t, at] = real
            src_im[t, at] = imag
            src_dif[t, at] = real - imag
        return carry

    lax.fori_loop(0, SEG, widen, 0)
    blank = jnp.zeros((6 * SB, F), jnp.float32)
    src_re[SEG] = blank
    src_im[SEG] = blank
    src_dif[SEG] = blank

    def one_source(s, carry):
        base = (s // SB) * 3 * SB + lax.rem(s, SB)
        for group in range(G):
            steps = (zeros if group == 0 else ones) + UNROLL - 1
            for tile in range(3):

                def walk(step, sums):
                    sums = list(sums)
                    for turn in range(UNROLL):
                        t = order[group, step * UNROLL + turn]
                        at = jnp.minimum(t, SEG - 1)
                        rec = []
                        for comp in range(3):
                            place = pl.ds(tile * 8, 8)
                            rec.append(
                                (rec_re[at, comp, place], rec_im[at, comp, place], rec_sum[at, comp, place])
                            )
                        for a in range(3):
                            row = pl.ds(base + a * SB, 8, stride=0)
                            src = (src_re[t, row], src_im[t, row], src_dif[t, row])
                            for b in range(3):
                                for k in range(3):
                                    i = (a * 3 + b) * 3 + k
                                    sums[i] = sums[i] + src[k] * rec[b][k]
                    return tuple(sums)

                zero = jnp.zeros((8, F), jnp.float32)
                sums = lax.fori_loop(0, steps // UNROLL, walk, (zero,) * 27)
                for c in range(9):
                    one, two, three = sums[3 * c : 3 * c + 3]
                    row = ((group * 3 + tile) * 9 + c) * 8
                    cross[row : row + 8, 0:F] = one + two
                    cross[row : row + 8, F : 2 * F] = three - one + two
        both = cross[...]
        upper = both.astype(jnp.bfloat16)
        lower = (both - upper.astype(jnp.float32)).astype(jnp.bfloat16)
        high = high_ref[...]
        product = jnp.dot(upper, low_ref[...], preferred_element_type=jnp.float32)
        product += jnp.dot(lower, high, preferred_element_type=jnp.float32)
        product += jnp.dot(upper, high, preferred_element_type=jnp.float32)
        lagged[...] = product
        for group in range(G):
            hits = (group_tile_ref[...] == group).astype(jnp.float32)
            scale = lax.rsqrt(jnp.sum(hits, keepdims=True))
            for q in range(4):
                to = owner_ref[4 * s + q]
                for c in range(9):
                    r = q * PB
                    while r < (q + 1) * PB:
                        tile, inside = divmod(r, 8)
                        count = min(8 - inside, (q + 1) * PB - r)
                        row = ((group * 3 + tile) * 9 + c) * 8 + inside
                        put = (group * 9 + c) * PB + r - q * PB
                        out_ref[to, put : put + count] = lagged[row : row + count] * scale
                        r += count
        return carry

    lax.fori_loop(0, S, one_source, 0)


def stack(day, group_of, owner, spectra, sources):
    high, low = lag_tables()
    vmem = pl.BlockSpec(memory_space=pltpu.VMEM)
    smem = pl.BlockSpec(memory_space=pltpu.SMEM)
    rec = pltpu.VMEM((SEG, 3, R, F), jnp.float32)
    src = pltpu.VMEM((SEG + 1, 6 * SB, F), jnp.float32)
    return pl.pallas_call(
        stack_kernel,
        out_shape=jax.ShapeDtypeStruct((N_DAY, ROWS, LAG), jnp.float32),
        in_specs=[smem, smem, smem, vmem, vmem, vmem, vmem, vmem],
        out_specs=vmem,
        scratch_shapes=[
            rec, rec, rec, src, src, src,
            pltpu.VMEM((G * 3 * 9 * 8, 2 * F), jnp.float32),
            pltpu.VMEM((G * 3 * 9 * 8, LAG), jnp.float32),
            pltpu.SMEM((G, SEG + UNROLL), jnp.int32),
        ],
        compiler_params=pltpu.CompilerParams(vmem_limit_bytes=VMEM_LIMIT),
        name="stack",
    )(
        day, group_of, owner, group_of.reshape(-1, 128), spectra, sources,
        jnp.asarray(high), jnp.asarray(low),
    )


def reduce_kernel(part_ref, out_ref, slots, y_mine, y_slots, z_send, z_recv, y_send, y_recv):
    day = lax.axis_index("day")
    z, y = day // N_Y, lax.rem(day, N_Y)

    def owner(dz, dy):
        return lax.rem(z + dz + N_Z, N_Z) * N_Y + lax.rem(y + dy, N_Y)

    barrier = pltpu.get_barrier_semaphore()
    partners = [owner(1, 0), owner(-1, 0)] + [owner(0, dy) for dy in range(1, N_Y)]
    for to in partners:
        pl.semaphore_signal(barrier, inc=1, device_id={"day": to}, device_id_type=MESH)
    pl.semaphore_wait(barrier, len(partners))

    half = N_Z // 2
    order = (2, 1, 3, 0)
    opening = ((2, 1), (3, 0))
    copies = {}

    def hop(way, step, dy, source):
        copy = pltpu.make_async_remote_copy(
            src_ref=source,
            dst_ref=slots.at[way, step, dy],
            send_sem=z_send.at[way, step, dy],
            recv_sem=z_recv.at[way, step, dy],
            device_id={"day": owner(1 - 2 * way, 0)},
            device_id_type=MESH,
        )
        copy.start()
        copies[way, step, dy] = copy

    for step in range(half):
        for dy in order:
            for way in range(2):
                dz = (half - step) * (1 - 2 * way)
                own = owner(dz, dy)
                if step == 0:
                    if dy in opening[way]:
                        hop(way, step, dy, part_ref.at[own])
                elif (way, step - 1, dy) in copies:
                    copies[way, step - 1, dy].wait_recv()
                    slots[way, step - 1, dy] += part_ref[own]
                    hop(way, step, dy, slots.at[way, step - 1, dy])
                else:
                    hop(way, step, dy, part_ref.at[own])
    y_copies = []
    for dy in order:
        for way in range(2):
            copies[way, half - 1, dy].wait_recv()
        total = part_ref[owner(0, dy)] + slots[0, half - 1, dy] + slots[1, half - 1, dy]
        y_mine[dy] = total
        if dy:
            copy = pltpu.make_async_remote_copy(
                src_ref=y_mine.at[dy],
                dst_ref=y_slots.at[dy - 1],
                send_sem=y_send.at[dy - 1],
                recv_sem=y_recv.at[dy - 1],
                device_id={"day": owner(0, dy)},
                device_id_type=MESH,
            )
            copy.start()
            y_copies.append(copy)
    for copy in y_copies:
        copy.wait_recv()
    total = y_mine[0] + y_slots[0] + y_slots[1] + y_slots[2]
    for group in range(G):
        for c in range(9):
            row = (group * 9 + c) * PB
            for r in range(PB):
                out_ref[r, c, group : group + 1, :] = total[row + r : row + r + 1]
    for copy in list(copies.values()) + y_copies:
        copy.wait_send()


def reduce(part):
    half = N_Z // 2
    chunk = (ROWS, LAG)
    return pl.pallas_call(
        reduce_kernel,
        out_shape=jax.ShapeDtypeStruct((PB, 9, G, LAG), jnp.float32),
        in_specs=[pl.BlockSpec(memory_space=pltpu.VMEM)],
        out_specs=pl.BlockSpec(memory_space=pltpu.VMEM),
        scratch_shapes=[
            pltpu.VMEM((2, half, N_Y) + chunk, jnp.float32),
            pltpu.VMEM((N_Y,) + chunk, jnp.float32),
            pltpu.VMEM((N_Y - 1,) + chunk, jnp.float32),
            pltpu.SemaphoreType.DMA((2, half, N_Y)),
            pltpu.SemaphoreType.DMA((2, half, N_Y)),
            pltpu.SemaphoreType.DMA((N_Y - 1,)),
            pltpu.SemaphoreType.DMA((N_Y - 1,)),
        ],
        compiler_params=pltpu.CompilerParams(
            collective_id=1, has_side_effects=True, vmem_limit_bytes=VMEM_LIMIT
        ),
        name="reduce",
    )(part)


def local(spectra, src_block, group_of, owner):
    sources = share(src_block, spectra)
    day = lax.axis_index("day").astype(jnp.int32).reshape(1)
    part = stack(day, group_of, owner, spectra, sources)
    return reduce(part).transpose(0, 2, 1, 3)[None]


def solution(mesh):
    return jax.shard_map(
        local,
        mesh=mesh,
        in_specs=(P("day", None, None, "sta", None), P(), P(), P()),
        out_specs=P("day", "sta", None, None, None),
        check_vma=False,
    )
```

time: 547 us -> 85.9 us (0.16)
  the two profiles are of different devices: /device:TPU:6 before, /device:TPU:1 now
where the time goes in v1:
time: 85.9 us; the launch traced here: 85.7 us
  Pallas kernels  82.7 us (96%)
  local copies, waits for them, and re-layouts  2.99 us (3%)
    pallas_call x1, Pallas kernels, reduce(): pl.pallas_call(reduce_kernel, out_shape=jax.ShapeDtypeStruct((PB, 9, G, L...  33.8 us
    pallas_call x1, Pallas kernels, share(): pl.pallas_call(share_kernel, out_shape=jax.ShapeDtypeStruct((N_STA, 2, PI...  25.7 us
    pallas_call x1, Pallas kernels, stack(): pl.pallas_call(stack_kernel, out_shape=jax.ShapeDtypeStruct((N_DAY, ROWS,...  23.1 us
    unnamed x15, local copies, waits for them, and re-layouts  2.99 us

profile of v1, /device:TPU:1, one launch (start us, length us, event | category | flops | bytes accessed | tf_op | source)
XLA Modules:
  0.0 85.7 jit_solution(11295452898496073169)
XLA Ops:
  0.0 0.0 copy-start.4
  0.0 0.0 copy-start.5
  0.0 0.0 copy-start
  0.0 1.7 %copy-done = bf16[64,2,3,24,128]{4,3,2,1,0:T(8,128)(2,1)S(1)} copy-done((bf16[64,2,3,24,128]{4,3,2,1,0:T(8,128)(2,1)S(1)}, bf16[64,2,3,24,128]{4,3,2,1,0:T(8,128)(2,1)}, u32[]{:S(2)}) %copy-start) | copy-done | bytes 2359320
  1.7 0.0 copy-start.6
  1.7 0.7 copy-done.6
  2.4 0.0 copy-start.1
  2.4 0.0 copy-start.2
  2.4 0.0 copy-start.3
  2.4 25.7 %share.1.source_ref = bf16[16,2,4,24,128]{4,3,2,1,0:T(8,128)(2,1)S(1)} custom-call(s32[2]{0:T(128)S(1)} %copy-done.6, bf16[16,4,2,3,24,128]{5,4,3,2,1,0:T(8,128)(2,1)S(1)} %bitcast.6), custom_call_target="tpu_custom_call" | custom-call | tf_op jit(solution)/shard_map/share/pallas_call | solution.py:120
  28.1 0.0 copy-done.4
  28.1 0.0 copy-done.5
  28.1 0.0 copy-done.1
  28.1 0.0 copy-done.2
  28.1 0.0 copy-done.3
  28.2 23.1 %stack.1.part_ref = f32[32,112,128]{2,1,0:T(8,128)S(1)} custom-call(s32[1]{0:T(128)} %bitcast.day_ref, s32[2048]{0:T(1024)S(1)} %copy-done.4, s32[32]{0:T(128)S(1)} %copy-done.5, s32[16,128]{1,0:T(8,128)S(1)} %bitcast.8, bf16[64,2,3,24,128]{4,3,2,1,0:T(8,128)(2,1)S(1)} %copy-done.1, bf16[16,2,4,24,128]{4,3,2,1,0:T(8,128)(2,1)S(1)} %share.1.source_ref, ...), custom_call_target="tpu_custom_call" | custom-call | tf_op jit(solution)/shard_map/stack/pallas_call | solution.py:256
  51.3 33.8 %reduce.1 = f32[6,9,2,128]{3,2,1,0:T(2,128)S(1)} custom-call(f32[32,112,128]{2,1,0:T(8,128)S(1)} %stack.1.part_ref), custom_call_target="tpu_custom_call" | custom-call | tf_op jit(solution)/shard_map/reduce/pallas_call | solution.py:351
  85.1 0.6 copy.8
Async XLA Ops:
  0.0 28.1 %copy-start.4 = (s32[2048]{0:T(1024)S(1)}, s32[2048]{0:T(1024)}, u32[]{:S(2)}) copy-start(s32[2048]{0:T(1024)} %group_ref.1) | copy-start | bytes 24580
  0.0 28.1 %copy-start.5 = (s32[32]{0:T(128)S(1)}, s32[32]{0:T(128)}, u32[]{:S(2)}) copy-start(s32[32]{0:T(128)} %owner_ref.1) | copy-start | bytes 388
  0.0 1.7 %copy-start = (bf16[64,2,3,24,128]{4,3,2,1,0:T(8,128)(2,1)S(1)}, bf16[64,2,3,24,128]{4,3,2,1,0:T(8,128)(2,1)}, u32[]{:S(2)}) copy-start(bf16[64,2,3,24,128]{4,3,2,1,0:T(8,128)(2,1)} %spec_ref.1) | copy-start | bytes 7077892
  1.7 0.7 copy-start.6
  2.4 25.8 %copy-start.1 = (bf16[64,2,3,24,128]{4,3,2,1,0:T(8,128)(2,1)S(1)}, bf16[64,2,3,24,128]{4,3,2,1,0:T(8,128)(2,1)}, u32[]{:S(2)}) copy-start(bf16[64,2,3,24,128]{4,3,2,1,0:T(8,128)(2,1)} %spec_ref.1) | copy-start | bytes 7077892
  2.4 25.8 %copy-start.2 = (bf16[256,128]{1,0:T(8,128)(2,1)S(1)}, bf16[256,128]{1,0:T(8,128)(2,1)}, u32[]{:S(2)}) copy-start(bf16[256,128]{1,0:T(8,128)(2,1)} %constant.11.clone.low_ref) | copy-start | bytes 196612
  2.4 25.8 %copy-start.3 = (bf16[256,128]{1,0:T(8,128)(2,1)S(1)}, bf16[256,128]{1,0:T(8,128)(2,1)}, u32[]{:S(2)}) copy-start(bf16[256,128]{1,0:T(8,128)(2,1)} %constant.10.clone.high_ref) | copy-start | bytes 196612

commit v2 on v0

v2 whole, which is shorter than its diff:
```python
import jax
import jax.numpy as jnp
import numpy as np
from jax import lax
from jax.experimental import pallas as pl
from jax.experimental.pallas import tpu as pltpu
from jax.sharding import PartitionSpec as P

F = 128
LAG = 128
G = 2
SB = 4
S = 8
PB = 6
SEG = 64
R = 24
N_STA = 16
N_DAY = 32
N_Z = 8
N_Y = 4
HALF_Z = N_Z // 2
PIECE = SEG // N_STA
CHUNK = 4
N_CHUNK = SEG // CHUNK + 1
ROWS = 40
MESH = pl.DeviceIdType.MESH
VMEM_LIMIT = 56 * 1024 * 1024


def lag_tables():
    freq = np.arange(F)
    lag = np.arange(LAG) - LAG // 2
    angle = 2.0 * np.pi / (2 * F) * np.mod(freq[:, None] * lag[None, :], 2 * F)
    weight = np.where(freq == 0, 1.0, 2.0) / np.sqrt(F)
    table = np.concatenate(
        [weight[:, None] * np.cos(angle), -weight[:, None] * np.sin(angle)], axis=0
    )
    high = table.astype(jnp.bfloat16)
    low = (table - high.astype(np.float64)).astype(jnp.bfloat16)
    return np.concatenate([high, low], axis=1)


def plan_kernel(day_ref, group_ref, owner_ref, tile_ref, order_ref, block_ref, scale_ref):
    first = day_ref[0] * SEG

    def clear(i, carry):
        order_ref[i] = SEG
        return carry

    lax.fori_loop(0, N_CHUNK * CHUNK, clear, 0)
    ones = lax.fori_loop(0, SEG, lambda t, n: n + group_ref[first + t], jnp.int32(0))
    chunks = (SEG - ones + CHUNK - 1) // CHUNK
    order_ref[N_CHUNK * CHUNK] = chunks

    def place(t, carry):
        early, late = carry
        group = group_ref[first + t]
        order_ref[jnp.where(group == 0, early, late)] = t
        return early + 1 - group, late + group

    lax.fori_loop(0, SEG, place, (jnp.int32(0), chunks * CHUNK))

    def turn(k, carry):
        block_ref[owner_ref[k]] = k
        return carry

    lax.fori_loop(0, N_DAY, turn, 0)
    for group in range(G):
        hits = (tile_ref[...] == group).astype(jnp.float32)
        scale_ref[group] = jnp.broadcast_to(lax.rsqrt(jnp.sum(hits, keepdims=True)), (8, LAG))


def plan(day, group_of, owner):
    vmem = pl.BlockSpec(memory_space=pltpu.VMEM)
    smem = pl.BlockSpec(memory_space=pltpu.SMEM)
    return pl.pallas_call(
        plan_kernel,
        out_shape=(
            jax.ShapeDtypeStruct((N_CHUNK * CHUNK + 4,), jnp.int32),
            jax.ShapeDtypeStruct((N_DAY,), jnp.int32),
            jax.ShapeDtypeStruct((G, 8, LAG), jnp.float32),
        ),
        in_specs=[smem, smem, smem, vmem],
        out_specs=(smem, smem, vmem),
        name="plan",
    )(day, group_of, owner, group_of.reshape(-1, 128))


def main_kernel(
    root_ref, order_ref, block_ref, scale_ref, table_ref, spec_ref, out_ref,
    spec, mine, seen, picked, rec_re, rec_im, rec_sum, src_re, src_im, src_dif, hist, cross, part,
    opening, slots, y_mine, y_slots,
    in_sem, a_send, a_recv, b_send, b_recv, c_send, c_recv, z_send, z_recv, y_send, y_recv,
):
    me = lax.axis_index("sta")
    partner = me + 1 - 2 * lax.rem(me, 2)
    day = lax.axis_index("day")
    z, y = day // N_Y, lax.rem(day, N_Y)
    rec = (rec_re, rec_im, rec_sum)
    src = (src_re, src_im, src_dif)

    def member(dz, dy):
        return lax.rem(z + dz + N_Z, N_Z) * N_Y + lax.rem(y + dy, N_Y)

    def push(source, target, send, recv, device):
        return pltpu.make_async_remote_copy(
            src_ref=source, dst_ref=target, send_sem=send, recv_sem=recv,
            device_id=device, device_id_type=MESH,
        )

    started = []

    fetch = [
        pltpu.make_async_copy(
            spec_ref.at[:, :, :, :, pl.ds(at, n), :], spec.at[:, :, :, :, pl.ds(at, n), :], in_sem.at[i]
        )
        for i, (at, n) in enumerate(((0, 8), (8, R - 8)))
    ]
    for copy in fetch:
        copy.start()
    barrier = pltpu.get_barrier_semaphore()
    for step in range(1, N_STA):
        pl.semaphore_signal(
            barrier, inc=1, device_id={"sta": lax.rem(me + step, N_STA)}, device_id_type=MESH
        )
    near = [member(1, 0), member(-1, 0)] + [member(0, dy) for dy in range(1, N_Y)]
    for to in near:
        pl.semaphore_signal(barrier, inc=1, device_id={"day": to}, device_id_type=MESH)
    fetch[0].wait()
    for p in range(2):
        for comp in range(3):
            row = (p * 3 + comp) * SB
            mine[:, :, row : row + SB, :] = spec[:, :, p, comp, 0:SB, :]
    pl.semaphore_wait(barrier, N_STA - 1 + len(near))
    scatters = []
    for step in range(1, N_STA):
        to = lax.rem(me + step, N_STA)
        scatters.append(
            push(mine.at[to], seen.at[me], a_send.at[step - 1], a_recv.at[step - 1], {"sta": to})
        )
        scatters[-1].start()
    seen[me] = mine[me]
    fetch[1].wait()

    def widen_rec(j, carry):
        for i in range(PIECE):
            for comp in range(3):
                real = spec[j, i, 0, comp].astype(jnp.float32)
                imag = spec[j, i, 1, comp].astype(jnp.float32)
                rec_re[j * PIECE + i, comp] = real
                rec_im[j * PIECE + i, comp] = imag
                rec_sum[j * PIECE + i, comp] = real + imag
        return carry

    lax.fori_loop(0, N_STA, widen_rec, 0)
    for k in range(3):
        rec[k][SEG] = jnp.zeros((3, R, F), jnp.float32)
        src[k][SEG] = jnp.zeros((6 * SB, F), jnp.float32)
    hist[0] = jnp.zeros((3 * SB, 3, 8, F), jnp.float32)
    for copy in scatters:
        copy.wait_recv()
    for block in range(2):
        picked[me, block] = seen[root_ref[block]]
    half = N_STA // 2
    spreads, hands = [], []
    for step in range(1, half):
        to = lax.rem(me + 2 * step, N_STA)
        spreads.append(
            push(picked.at[me], picked.at[me], b_send.at[step - 1], b_recv.at[step - 1], {"sta": to})
        )
        spreads[-1].start()
    for step in range(half):
        if step:
            spreads[step - 1].wait_recv()
        piece = picked.at[lax.rem(me + N_STA - 2 * step, N_STA)]
        hands.append(push(piece, piece, c_send.at[step], c_recv.at[step], {"sta": partner}))
        hands[-1].start()
    for copy in hands:
        copy.wait_recv()
    started += scatters + spreads + hands

    def widen_src(j, carry):
        for i in range(PIECE):
            for block in range(2):
                rows = picked[j, block, i].astype(jnp.float32)
                real, imag = rows[: 3 * SB], rows[3 * SB :]
                at = pl.ds(block * 3 * SB, 3 * SB)
                src_re[j * PIECE + i, at] = real
                src_im[j * PIECE + i, at] = imag
                src_dif[j * PIECE + i, at] = real - imag
        return carry

    lax.fori_loop(0, N_STA, widen_src, 0)

    def unit(a, block, tile):
        place = pl.ds(tile * 8, 8)
        sums = [jnp.zeros((3, 8, F), jnp.float32)] * (3 * SB)
        for chunk in range(N_CHUNK):
            for turn in range(CHUNK):
                t = order_ref[chunk * CHUNK + turn]
                held = [rec[k][t, :, place] for k in range(3)]
                for s in range(SB):
                    row = pl.ds((block * 3 + a) * SB + s, 8, stride=0)
                    for k in range(3):
                        sums[s * 3 + k] = sums[s * 3 + k] + src[k][t, row][None] * held[k]
            for i in range(3 * SB):
                hist[chunk + 1, i] = sums[i]
        cut = order_ref[N_CHUNK * CHUNK]
        for s in range(SB):
            early = [hist[cut, 3 * s + k] for k in range(3)]
            late = [sums[3 * s + k] - early[k] for k in range(3)]
            for group, (one, two, three) in enumerate((early, late)):
                cross[group, s, :, :, 0:F] = one + two
                cross[group, s, :, :, F : 2 * F] = three - one + two
        both = cross[...].reshape(G * SB * 3 * 8, 2 * F)
        upper = both.astype(jnp.bfloat16)
        lower = (both - upper.astype(jnp.float32)).astype(jnp.bfloat16)
        wide = jnp.dot(upper, table_ref[...], preferred_element_type=jnp.float32)
        narrow = jnp.dot(lower, table_ref[:, 0:LAG], preferred_element_type=jnp.float32)
        lagged = (wide[:, :LAG] + wide[:, LAG:] + narrow).reshape(G, SB, 3, 8, LAG)
        for group in range(G):
            for s in range(SB):
                for b in range(3):
                    rows = lagged[group, s, b] * scale_ref[group]
                    r = tile * 8
                    while r < tile * 8 + 8:
                        q, inside = divmod(r, PB)
                        count = min(PB - inside, tile * 8 + 8 - r)
                        put = (group * 3 + b) * PB + inside
                        at = r - tile * 8
                        part[a, (block * SB + s) * 4 + q, put : put + count] = rows[at : at + count]
                        r += count

    def own(a, dz, dy):
        return part[a, block_ref[member(dz, dy)]]

    chains = {}

    def hop(a, step):
        for way in range(2):
            dz = (HALF_Z - step) * (1 - 2 * way)
            to = {"day": member(1 - 2 * way, 0)}
            sems = (z_send.at[a, way, step], z_recv.at[a, way, step])
            if step == 0:
                for i in range(2):
                    opening[a, way, i] = own(a, dz, 2 * way + i)
                copy = push(
                    opening.at[a, way], slots.at[a, way, 0, pl.ds(2 * way, 2)], *sems, to
                )
            else:
                chains[a, way, step - 1].wait_recv()
                for dy in range(N_Y):
                    if step == 1 and dy // 2 != way:
                        slots[a, way, 0, dy] = own(a, dz, dy)
                    else:
                        slots[a, way, step - 1, dy] += own(a, dz, dy)
                copy = push(slots.at[a, way, step - 1], slots.at[a, way, step], *sems, to)
            copy.start()
            chains[a, way, step] = copy
            started.append(copy)

    crossings = {}

    def across(a):
        for way in range(2):
            chains[a, way, HALF_Z - 1].wait_recv()
        for dy in (2, 1, 3, 0):
            y_mine[a, dy] = own(a, 0, dy) + slots[a, 0, HALF_Z - 1, dy] + slots[a, 1, HALF_Z - 1, dy]
            if dy:
                copy = push(
                    y_mine.at[a, dy], y_slots.at[a, dy - 1],
                    y_send.at[a, dy - 1], y_recv.at[a, dy - 1], {"day": member(0, dy)},
                )
                copy.start()
                crossings[a, dy] = copy
                started.append(copy)

    def finish(a):
        for dy in range(1, N_Y):
            crossings[a, dy].wait_recv()
        total = y_mine[a, 0] + y_slots[a, 0] + y_slots[a, 1] + y_slots[a, 2]
        for group in range(G):
            for b in range(3):
                row = (group * 3 + b) * PB
                for r in range(PB):
                    out_ref[r, 3 * a + b, group : group + 1, :] = total[row + r : row + r + 1]

    def twice(a, tile):
        def body(block, carry):
            unit(a, block, tile)
            return carry

        lax.fori_loop(0, 2, body, 0)

    for tile in range(3):
        twice(0, tile)
    hop(0, 0)
    twice(1, 0)
    hop(0, 1)
    twice(1, 1)
    hop(0, 2)
    twice(1, 2)
    hop(0, 3)
    hop(1, 0)
    twice(2, 0)
    hop(1, 1)
    across(0)
    twice(2, 1)
    hop(1, 2)
    finish(0)
    twice(2, 2)
    hop(2, 0)
    hop(1, 3)
    hop(2, 1)
    across(1)
    hop(2, 2)
    finish(1)
    hop(2, 3)
    across(2)
    finish(2)
    for copy in started:
        copy.wait_send()


def main(src_block, order, block_at, scale, spectra):
    pieces = spectra.reshape(N_STA, PIECE, 2, 3, R, F)
    half = N_STA // 2
    vmem = pl.BlockSpec(memory_space=pltpu.VMEM)
    smem = pl.BlockSpec(memory_space=pltpu.SMEM)
    dma = pltpu.SemaphoreType.DMA
    rec = pltpu.VMEM((SEG + 1, 3, R, F), jnp.float32)
    src = pltpu.VMEM((SEG + 1, 6 * SB, F), jnp.float32)
    rows = pltpu.VMEM((N_STA, PIECE, 6 * SB, F), jnp.bfloat16)
    chunk = (ROWS, LAG)
    return pl.pallas_call(
        main_kernel,
        out_shape=jax.ShapeDtypeStruct((PB, 9, G, LAG), jnp.float32),
        in_specs=[smem, smem, smem, vmem, vmem, pl.BlockSpec(memory_space=pl.ANY)],
        out_specs=vmem,
        scratch_shapes=[
            pltpu.VMEM(pieces.shape, jnp.bfloat16),
            rows, rows,
            pltpu.VMEM((N_STA, 2, PIECE, 6 * SB, F), jnp.bfloat16),
            rec, rec, rec, src, src, src,
            pltpu.VMEM((N_CHUNK + 1, 3 * SB, 3, 8, F), jnp.float32),
            pltpu.VMEM((G, SB, 3, 8, 2 * F), jnp.float32),
            pltpu.VMEM((3, N_DAY) + chunk, jnp.float32),
            pltpu.VMEM((3, 2, 2) + chunk, jnp.float32),
            pltpu.VMEM((3, 2, HALF_Z, N_Y) + chunk, jnp.float32),
            pltpu.VMEM((3, N_Y) + chunk, jnp.float32),
            pltpu.VMEM((3, N_Y - 1) + chunk, jnp.float32),
            dma((2,)),
            dma((N_STA - 1,)), dma((N_STA - 1,)),
            dma((half - 1,)), dma((half - 1,)),
            dma((half,)), dma((half,)),
            dma((3, 2, HALF_Z)), dma((3, 2, HALF_Z)),
            dma((3, N_Y - 1)), dma((3, N_Y - 1)),
        ],
        compiler_params=pltpu.CompilerParams(
            collective_id=0, has_side_effects=True, vmem_limit_bytes=VMEM_LIMIT
        ),
        name="main",
    )(src_block, order, block_at, scale, jnp.asarray(lag_tables()), pieces)


def local(spectra, src_block, group_of, owner):
    day = lax.axis_index("day").astype(jnp.int32).reshape(1)
    order, block_at, scale = plan(day, group_of, owner)
    return main(src_block, order, block_at, scale, spectra).transpose(0, 2, 1, 3)[None]


def solution(mesh):
    return jax.shard_map(
        local,
        mesh=mesh,
        in_specs=(P("day", None, None, "sta", None), P(), P(), P()),
        out_specs=P("day", "sta", None, None, None),
        check_vma=False,
    )
```

time: 547 us -> 83.8 us (0.15)
  the two profiles are of different devices: /device:TPU:6 before, /device:TPU:8 now
where the time goes in v2:
time: 83.8 us; the launch traced here: 83.5 us
  Pallas kernels  82.1 us (98%)
  local copies, waits for them, and re-layouts  1.44 us (2%)
    pallas_call x1, Pallas kernels, main(): pl.pallas_call(main_kernel, out_shape=jax.ShapeDtypeStruct((PB, 9, G, LAG...  78.7 us
    pallas_call x1, Pallas kernels, plan(): pl.pallas_call(plan_kernel, out_shape=(jax.ShapeDtypeStruct((N_CHUNK * CH...  3.37 us

profile of v2, /device:TPU:8, one launch (start us, length us, event | category | flops | bytes accessed | tf_op | source)
XLA Modules:
  0.0 83.5 jit_solution(4015873143921977356)
XLA Ops:
  0.0 3.4 %plan.1 = (s32[72]{0:T(128)}, s32[32]{0:T(128)}, f32[2,8,128]{2,1,0:T(8,128)}) custom-call(s32[1]{0:T(128)} %bitcast.day_ref, s32[2048]{0:T(1024)} %group_ref.1, s32[32]{0:T(128)} %owner_ref.1, s32[16,128]{1,0:T(8,128)} %bitcast.8), custom_call_target="tpu_custom_call" | custom-call | tf_op jit(solution)/shard_map/plan/pallas_call | solution.py:76
  3.4 78.7 %main.1 = f32[6,9,2,128]{3,2,1,0:T(2,128)} custom-call(s32[2]{0:T(128)} %root_ref.1, s32[72]{0:T(128)} %get-tuple-element.8.order_ref, s32[32]{0:T(128)} %get-tuple-element.9.block_ref, f32[2,8,128]{2,1,0:T(8,128)} %get-tuple-element.10.scale_ref, bf16[256,256]{1,0:T(8,128)(2,1)} %constant.8.clone.table_ref, bf16[16,4,2,3,24,128]{5,4,3,2,1,0:T(8,128)(2,1)} %bitcast.6), custom_call_target="tpu_custom_call" | custom-call | tf_op jit(solution)/shard_map/main/pallas_call | solution.py:335
  82.1 1.4 %copy.7 = f32[1,6,2,9,128]{4,2,3,1,0:T(2,128)} copy(f32[1,6,2,9,128]{4,2,3,1,0:T(2,128)} %bitcast.7) | data formatting | bytes 110592

commit v3 on v2

--- a/solution.py
+++ b/solution.py
@@ -16,13 +16,14 @@
 R = 24
 N_STA = 16
 N_DAY = 32
-N_Z = 8
-N_Y = 4
-HALF_Z = N_Z // 2
 PIECE = SEG // N_STA
 CHUNK = 4
 N_CHUNK = SEG // CHUNK + 1
 ROWS = 40
+CODED = 36
+STEPS = 256.0
+PEAK = 32767.0
+BATCH = 8
 MESH = pl.DeviceIdType.MESH
 VMEM_LIMIT = 56 * 1024 * 1024
 
@@ -47,8 +48,8 @@
         order_ref[i] = SEG
         return carry
 
-    lax.fori_loop(0, N_CHUNK * CHUNK, clear, 0)
-    ones = lax.fori_loop(0, SEG, lambda t, n: n + group_ref[first + t], jnp.int32(0))
+    lax.fori_loop(0, N_CHUNK * CHUNK, clear, 0, unroll=True)
+    ones = lax.fori_loop(0, SEG, lambda t, n: n + group_ref[first + t], jnp.int32(0), unroll=True)
     chunks = (SEG - ones + CHUNK - 1) // CHUNK
     order_ref[N_CHUNK * CHUNK] = chunks
 
@@ -58,13 +59,13 @@
         order_ref[jnp.where(group == 0, early, late)] = t
         return early + 1 - group, late + group
 
-    lax.fori_loop(0, SEG, place, (jnp.int32(0), chunks * CHUNK))
+    lax.fori_loop(0, SEG, place, (jnp.int32(0), chunks * CHUNK), unroll=True)
 
     def turn(k, carry):
         block_ref[owner_ref[k]] = k
         return carry
 
-    lax.fori_loop(0, N_DAY, turn, 0)
+    lax.fori_loop(0, N_DAY, turn, 0, unroll=True)
     for group in range(G):
         hits = (tile_ref[...] == group).astype(jnp.float32)
         scale_ref[group] = jnp.broadcast_to(lax.rsqrt(jnp.sum(hits, keepdims=True)), (8, LAG))
@@ -89,18 +90,13 @@
 def main_kernel(
     root_ref, order_ref, block_ref, scale_ref, table_ref, spec_ref, out_ref,
     spec, mine, seen, picked, rec_re, rec_im, rec_sum, src_re, src_im, src_dif, hist, cross, part,
-    opening, slots, y_mine, y_slots,
-    in_sem, a_send, a_recv, b_send, b_recv, c_send, c_recv, z_send, z_recv, y_send, y_recv,
+    coded, slots, in_sem, a_send, a_recv, b_send, b_recv, c_send, c_recv, d_send, d_recv,
 ):
     me = lax.axis_index("sta")
     partner = me + 1 - 2 * lax.rem(me, 2)
     day = lax.axis_index("day")
-    z, y = day // N_Y, lax.rem(day, N_Y)
     rec = (rec_re, rec_im, rec_sum)
     src = (src_re, src_im, src_dif)
-
-    def member(dz, dy):
-        return lax.rem(z + dz + N_Z, N_Z) * N_Y + lax.rem(y + dy, N_Y)
 
     def push(source, target, send, recv, device):
         return pltpu.make_async_remote_copy(
@@ -123,15 +119,16 @@
         pl.semaphore_signal(
             barrier, inc=1, device_id={"sta": lax.rem(me + step, N_STA)}, device_id_type=MESH
         )
-    near = [member(1, 0), member(-1, 0)] + [member(0, dy) for dy in range(1, N_Y)]
-    for to in near:
-        pl.semaphore_signal(barrier, inc=1, device_id={"day": to}, device_id_type=MESH)
+    for step in range(1, N_DAY):
+        pl.semaphore_signal(
+            barrier, inc=1, device_id={"day": lax.rem(day + step, N_DAY)}, device_id_type=MESH
+        )
     fetch[0].wait()
     for p in range(2):
         for comp in range(3):
             row = (p * 3 + comp) * SB
             mine[:, :, row : row + SB, :] = spec[:, :, p, comp, 0:SB, :]
-    pl.semaphore_wait(barrier, N_STA - 1 + len(near))
+    pl.semaphore_wait(barrier, N_STA + N_DAY - 2)
     scatters = []
     for step in range(1, N_STA):
         to = lax.rem(me + step, N_STA)
@@ -231,54 +228,42 @@
                         part[a, (block * SB + s) * 4 + q, put : put + count] = rows[at : at + count]
                         r += count
 
-    def own(a, dz, dy):
-        return part[a, block_ref[member(dz, dy)]]
-
-    chains = {}
-
-    def hop(a, step):
-        for way in range(2):
-            dz = (HALF_Z - step) * (1 - 2 * way)
-            to = {"day": member(1 - 2 * way, 0)}
-            sems = (z_send.at[a, way, step], z_recv.at[a, way, step])
-            if step == 0:
-                for i in range(2):
-                    opening[a, way, i] = own(a, dz, 2 * way + i)
-                copy = push(
-                    opening.at[a, way], slots.at[a, way, 0, pl.ds(2 * way, 2)], *sems, to
-                )
-            else:
-                chains[a, way, step - 1].wait_recv()
-                for dy in range(N_Y):
-                    if step == 1 and dy // 2 != way:
-                        slots[a, way, 0, dy] = own(a, dz, dy)
-                    else:
-                        slots[a, way, step - 1, dy] += own(a, dz, dy)
-                copy = push(slots.at[a, way, step - 1], slots.at[a, way, step], *sems, to)
-            copy.start()
-            chains[a, way, step] = copy
-            started.append(copy)
-
-    crossings = {}
-
-    def across(a):
-        for way in range(2):
-            chains[a, way, HALF_Z - 1].wait_recv()
-        for dy in (2, 1, 3, 0):
-            y_mine[a, dy] = own(a, 0, dy) + slots[a, 0, HALF_Z - 1, dy] + slots[a, 1, HALF_Z - 1, dy]
-            if dy:
-                copy = push(
-                    y_mine.at[a, dy], y_slots.at[a, dy - 1],
-                    y_send.at[a, dy - 1], y_recv.at[a, dy - 1], {"day": member(0, dy)},
-                )
-                copy.start()
-                crossings[a, dy] = copy
-                started.append(copy)
+    lane = lax.broadcasted_iota(jnp.int32, (ROWS, LAG), 1)
+    line = lax.broadcasted_iota(jnp.int32, (ROWS, LAG), 0)
+    diagonal = lane == line
+
+    def parcel(a, step):
+        return push(
+            coded.at[a, step - 1], slots.at[a, step - 1],
+            d_send.at[a, step - 1], d_recv.at[a, step - 1],
+            {"day": lax.rem(day + step, N_DAY)},
+        )
+
+    def post(a):
+        for first in range(1, N_DAY, BATCH):
+            steps = range(first, min(first + BATCH, N_DAY))
+            for step in steps:
+                rows = part[a, block_ref[lax.rem(day + step, N_DAY)]]
+                largest = jnp.max(jnp.abs(rows), axis=1, keepdims=True)
+                level = jnp.ceil(jnp.log2(jnp.maximum(largest, 1e-30)) * STEPS)
+                values = rows * (jnp.exp2(level * (-1.0 / STEPS)) * PEAK)
+                levels = jnp.sum(jnp.where(diagonal, level, 0.0), axis=0, keepdims=True)
+                values = jnp.where(line == CODED, levels, values)
+                coded[a, step - 1] = jnp.round(values).astype(jnp.int32).astype(jnp.int16)
+            for step in steps:
+                parcel(a, step).start()
 
     def finish(a):
-        for dy in range(1, N_Y):
-            crossings[a, dy].wait_recv()
-        total = y_mine[a, 0] + y_slots[a, 0] + y_slots[a, 1] + y_slots[a, 2]
+        total = part[a, block_ref[day]]
+        for first in range(1, N_DAY, BATCH):
+            steps = range(first, min(first + BATCH, N_DAY))
+            for step in steps:
+                parcel(a, step).wait_recv()
+            for step in steps:
+                values = slots[a, step - 1].astype(jnp.int32).astype(jnp.float32)
+                levels = jnp.where(diagonal, values[CODED : CODED + 1], 0.0)
+                level = jnp.sum(levels, axis=1, keepdims=True)
+                total = total + values * (jnp.exp2(level * (1.0 / STEPS)) * (1.0 / PEAK))
         for group in range(G):
             for b in range(3):
                 row = (group * 3 + b) * PB
@@ -292,34 +277,21 @@
 
         lax.fori_loop(0, 2, body, 0)
 
-    for tile in range(3):
-        twice(0, tile)
-    hop(0, 0)
-    twice(1, 0)
-    hop(0, 1)
-    twice(1, 1)
-    hop(0, 2)
-    twice(1, 2)
-    hop(0, 3)
-    hop(1, 0)
-    twice(2, 0)
-    hop(1, 1)
-    across(0)
-    twice(2, 1)
-    hop(1, 2)
-    finish(0)
-    twice(2, 2)
-    hop(2, 0)
-    hop(1, 3)
-    hop(2, 1)
-    across(1)
-    hop(2, 2)
-    finish(1)
-    hop(2, 3)
-    across(2)
-    finish(2)
+    for a in range(3):
+        for tile in range(3):
+            twice(a, tile)
+        post(a)
+    for a in range(3):
+        finish(a)
     for copy in started:
         copy.wait_send()
+
+    def settle(j, carry):
+        for a in range(3):
+            parcel(a, 1 + j).wait_send()
+        return carry
+
+    lax.fori_loop(0, N_DAY - 1, settle, 0)
 
 
 def main(src_block, order, block_at, scale, spectra):
@@ -345,16 +317,13 @@
             pltpu.VMEM((N_CHUNK + 1, 3 * SB, 3, 8, F), jnp.float32),
             pltpu.VMEM((G, SB, 3, 8, 2 * F), jnp.float32),
             pltpu.VMEM((3, N_DAY) + chunk, jnp.float32),
-            pltpu.VMEM((3, 2, 2) + chunk, jnp.float32),
-            pltpu.VMEM((3, 2, HALF_Z, N_Y) + chunk, jnp.float32),
-            pltpu.VMEM((3, N_Y) + chunk, jnp.float32),
-            pltpu.VMEM((3, N_Y - 1) + chunk, jnp.float32),
+            pltpu.VMEM((3, N_DAY - 1) + chunk, jnp.int16),
+            pltpu.VMEM((3, N_DAY - 1) + chunk, jnp.int16),
             dma((2,)),
             dma((N_STA - 1,)), dma((N_STA - 1,)),
             dma((half - 1,)), dma((half - 1,)),
             dma((half,)), dma((half,)),
-            dma((3, 2, HALF_Z)), dma((3, 2, HALF_Z)),
-            dma((3, N_Y - 1)), dma((3, N_Y - 1)),
+            dma((3, N_DAY - 1)), dma((3, N_DAY - 1)),
         ],
         compiler_params=pltpu.CompilerParams(
             collective_id=0, has_side_effects=True, vmem_limit_bytes=VMEM_LIMIT

time: 83.8 us -> 74.4 us (0.89)
  the two profiles are of different devices: /device:TPU:8 before, /device:TPU:17 now
where the time goes in v3:
time: 74.4 us; the launch traced here: 74.1 us
  Pallas kernels  72.7 us (98%)
  local copies, waits for them, and re-layouts  1.44 us (2%)
    pallas_call x1, Pallas kernels, main(): pl.pallas_call(main_kernel, out_shape=jax.ShapeDtypeStruct((PB, 9, G, LAG...  71 us
    pallas_call x1, Pallas kernels, plan(): pl.pallas_call(plan_kernel, out_shape=(jax.ShapeDtypeStruct((N_CHUNK * CH...  1.7 us

profile of v3, /device:TPU:17, one launch (start us, length us, event | category | flops | bytes accessed | tf_op | source)
XLA Modules:
  0.0 74.1 jit_solution(10008060763789433883)
XLA Ops:
  0.0 1.7 %plan.1 = (s32[72]{0:T(128)}, s32[32]{0:T(128)}, f32[2,8,128]{2,1,0:T(8,128)}) custom-call(s32[1]{0:T(128)} %bitcast.day_ref, s32[2048]{0:T(1024)} %group_ref.1, s32[32]{0:T(128)} %owner_ref.1, s32[16,128]{1,0:T(8,128)} %bitcast.8), custom_call_target="tpu_custom_call" | custom-call | tf_op jit(solution)/shard_map/plan/pallas_call | solution.py:77
  1.7 71.0 %main.1 = f32[6,9,2,128]{3,2,1,0:T(2,128)} custom-call(s32[2]{0:T(128)} %root_ref.1, s32[72]{0:T(128)} %get-tuple-element.8.order_ref, s32[32]{0:T(128)} %get-tuple-element.9.block_ref, f32[2,8,128]{2,1,0:T(8,128)} %get-tuple-element.10.scale_ref, bf16[256,256]{1,0:T(8,128)(2,1)} %constant.8.clone.table_ref, bf16[16,4,2,3,24,128]{5,4,3,2,1,0:T(8,128)(2,1)} %bitcast.6), custom_call_target="tpu_custom_call" | custom-call | tf_op jit(solution)/shard_map/main/pallas_call | solution.py:307
  72.7 1.4 %copy.7 = f32[1,6,2,9,128]{4,2,3,1,0:T(2,128)} copy(f32[1,6,2,9,128]{4,2,3,1,0:T(2,128)} %bitcast.7) | data formatting | bytes 110592

commit v4 on v3

--- a/solution.py
+++ b/solution.py
@@ -19,8 +19,10 @@
 PIECE = SEG // N_STA
 CHUNK = 4
 N_CHUNK = SEG // CHUNK + 1
-ROWS = 40
-CODED = 36
+PAIR = G * PB
+ROUNDS = ((0, 1), (2, 3), (4, 5), (6, 7), (8,))
+ROWS = 2 * PAIR
+LAST = 16
 STEPS = 256.0
 PEAK = 32767.0
 BATCH = 8
@@ -90,7 +92,7 @@
 def main_kernel(
     root_ref, order_ref, block_ref, scale_ref, table_ref, spec_ref, out_ref,
     spec, mine, seen, picked, rec_re, rec_im, rec_sum, src_re, src_im, src_dif, hist, cross, part,
-    coded, slots, in_sem, a_send, a_recv, b_send, b_recv, c_send, c_recv, d_send, d_recv,
+    coded, slots, coded_last, slots_last, levels, in_sem, a_send, a_recv, b_send, b_recv, c_send, c_recv, d_send, d_recv,
 ):
     me = lax.axis_index("sta")
     partner = me + 1 - 2 * lax.rem(me, 2)
@@ -153,53 +155,63 @@
     for k in range(3):
         rec[k][SEG] = jnp.zeros((3, R, F), jnp.float32)
         src[k][SEG] = jnp.zeros((6 * SB, F), jnp.float32)
-    hist[0] = jnp.zeros((3 * SB, 3, 8, F), jnp.float32)
+    hist[0] = jnp.zeros((3 * SB, R, F), jnp.float32)
     for copy in scatters:
         copy.wait_recv()
     for block in range(2):
         picked[me, block] = seen[root_ref[block]]
     half = N_STA // 2
-    spreads, hands = [], []
-    for step in range(1, half):
+
+    def spread(block, step):
+        piece = picked.at[me, block]
         to = lax.rem(me + 2 * step, N_STA)
-        spreads.append(
-            push(picked.at[me], picked.at[me], b_send.at[step - 1], b_recv.at[step - 1], {"sta": to})
-        )
-        spreads[-1].start()
-    for step in range(half):
-        if step:
-            spreads[step - 1].wait_recv()
-        piece = picked.at[lax.rem(me + N_STA - 2 * step, N_STA)]
-        hands.append(push(piece, piece, c_send.at[step], c_recv.at[step], {"sta": partner}))
-        hands[-1].start()
-    for copy in hands:
-        copy.wait_recv()
-    started += scatters + spreads + hands
-
-    def widen_src(j, carry):
-        for i in range(PIECE):
-            for block in range(2):
+        return push(piece, piece, b_send.at[block, step - 1], b_recv.at[block, step - 1], {"sta": to})
+
+    def hand(block, step):
+        piece = picked.at[lax.rem(me + N_STA - 2 * step, N_STA), block]
+        return push(piece, piece, c_send.at[block, step], c_recv.at[block, step], {"sta": partner})
+
+    spreads = [[spread(block, step) for step in range(1, half)] for block in range(2)]
+    hands = [[hand(block, step) for step in range(half)] for block in range(2)]
+    for block in range(2):
+        for copy in spreads[block]:
+            copy.start()
+    started += scatters + spreads[0] + spreads[1] + hands[0] + hands[1]
+
+    def hand_over(block):
+        hands[block][0].start()
+        for step in range(1, half):
+            spreads[block][step - 1].wait_recv()
+            hands[block][step].start()
+
+    def take(block):
+        for copy in hands[block]:
+            copy.wait_recv()
+
+        def widen_src(j, carry):
+            for i in range(PIECE):
                 rows = picked[j, block, i].astype(jnp.float32)
                 real, imag = rows[: 3 * SB], rows[3 * SB :]
                 at = pl.ds(block * 3 * SB, 3 * SB)
                 src_re[j * PIECE + i, at] = real
                 src_im[j * PIECE + i, at] = imag
                 src_dif[j * PIECE + i, at] = real - imag
-        return carry
-
-    lax.fori_loop(0, N_STA, widen_src, 0)
-
-    def unit(a, block, tile):
-        place = pl.ds(tile * 8, 8)
-        sums = [jnp.zeros((3, 8, F), jnp.float32)] * (3 * SB)
+            return carry
+
+        lax.fori_loop(0, N_STA, widen_src, 0)
+
+    def unit(pair, block):
+        a, b = divmod(pair, 3)
+        sums = [jnp.zeros((R, F), jnp.float32)] * (3 * SB)
         for chunk in range(N_CHUNK):
             for turn in range(CHUNK):
                 t = order_ref[chunk * CHUNK + turn]
-                held = [rec[k][t, :, place] for k in range(3)]
+                held = [rec[k][t, b].reshape(3, 8, F) for k in range(3)]
                 for s in range(SB):
                     row = pl.ds((block * 3 + a) * SB + s, 8, stride=0)
                     for k in range(3):
-                        sums[s * 3 + k] = sums[s * 3 + k] + src[k][t, row][None] * held[k]
+                        product = src[k][t, row][None] * held[k]
+                        sums[s * 3 + k] = sums[s * 3 + k] + product.reshape(R, F)
             for i in range(3 * SB):
                 hist[chunk + 1, i] = sums[i]
         cut = order_ref[N_CHUNK * CHUNK]
@@ -207,88 +219,106 @@
             early = [hist[cut, 3 * s + k] for k in range(3)]
             late = [sums[3 * s + k] - early[k] for k in range(3)]
             for group, (one, two, three) in enumerate((early, late)):
-                cross[group, s, :, :, 0:F] = one + two
-                cross[group, s, :, :, F : 2 * F] = three - one + two
-        both = cross[...].reshape(G * SB * 3 * 8, 2 * F)
+                cross[group, s, :, 0:F] = one + two
+                cross[group, s, :, F : 2 * F] = three - one + two
+        both = cross[...].reshape(G * SB * R, 2 * F)
         upper = both.astype(jnp.bfloat16)
         lower = (both - upper.astype(jnp.float32)).astype(jnp.bfloat16)
         wide = jnp.dot(upper, table_ref[...], preferred_element_type=jnp.float32)
         narrow = jnp.dot(lower, table_ref[:, 0:LAG], preferred_element_type=jnp.float32)
-        lagged = (wide[:, :LAG] + wide[:, LAG:] + narrow).reshape(G, SB, 3, 8, LAG)
+        lagged = (wide[:, :LAG] + wide[:, LAG:] + narrow).reshape(G, SB, R, LAG)
         for group in range(G):
+            scale = scale_ref[group, 0:1]
+            put = (pair % 2 * G + group) * PB
             for s in range(SB):
-                for b in range(3):
-                    rows = lagged[group, s, b] * scale_ref[group]
-                    r = tile * 8
-                    while r < tile * 8 + 8:
-                        q, inside = divmod(r, PB)
-                        count = min(PB - inside, tile * 8 + 8 - r)
-                        put = (group * 3 + b) * PB + inside
-                        at = r - tile * 8
-                        part[a, (block * SB + s) * 4 + q, put : put + count] = rows[at : at + count]
-                        r += count
+                rows = lagged[group, s] * scale
+                for q in range(R // PB):
+                    part[pair // 2, (block * SB + s) * 4 + q, put : put + PB] = rows[q * PB : (q + 1) * PB]
 
     lane = lax.broadcasted_iota(jnp.int32, (ROWS, LAG), 1)
     line = lax.broadcasted_iota(jnp.int32, (ROWS, LAG), 0)
-    diagonal = lane == line
-
-    def parcel(a, step):
+    end = len(ROUNDS) - 1
+    height = [ROWS] * end + [LAST]
+    diagonal = [(lane == line + n * ROWS)[: height[n]] for n in range(end + 1)]
+
+    def parcel(n, step):
+        source, target = (coded_last, slots_last) if n == end else (coded.at[n], slots.at[n])
         return push(
-            coded.at[a, step - 1], slots.at[a, step - 1],
-            d_send.at[a, step - 1], d_recv.at[a, step - 1],
+            source.at[step - 1], target.at[step - 1], d_send.at[n, step - 1], d_recv.at[n, step - 1],
             {"day": lax.rem(day + step, N_DAY)},
         )
 
-    def post(a):
+    def post(n):
         for first in range(1, N_DAY, BATCH):
             steps = range(first, min(first + BATCH, N_DAY))
             for step in steps:
-                rows = part[a, block_ref[lax.rem(day + step, N_DAY)]]
+                rows = part[n, block_ref[lax.rem(day + step, N_DAY)], 0 : height[n]]
                 largest = jnp.max(jnp.abs(rows), axis=1, keepdims=True)
                 level = jnp.ceil(jnp.log2(jnp.maximum(largest, 1e-30)) * STEPS)
                 values = rows * (jnp.exp2(level * (-1.0 / STEPS)) * PEAK)
-                levels = jnp.sum(jnp.where(diagonal, level, 0.0), axis=0, keepdims=True)
-                values = jnp.where(line == CODED, levels, values)
-                coded[a, step - 1] = jnp.round(values).astype(jnp.int32).astype(jnp.int16)
+                if n == end:
+                    level, at = level[:PAIR], diagonal[n][:PAIR]
+                else:
+                    at = diagonal[n]
+                mine_levels = jnp.sum(jnp.where(at, level, 0.0), axis=0, keepdims=True)
+                if n:
+                    mine_levels += levels[step - 1]
+                if n < end:
+                    levels[step - 1] = mine_levels
+                    coded[n, step - 1] = jnp.round(values).astype(jnp.int32).astype(jnp.int16)
+                else:
+                    values = jnp.where(line[:LAST] == PAIR, mine_levels, values)
+                    coded_last[step - 1] = jnp.round(values).astype(jnp.int32).astype(jnp.int16)
             for step in steps:
-                parcel(a, step).start()
-
-    def finish(a):
-        total = part[a, block_ref[day]]
+                parcel(n, step).start()
+
+    def finish():
+        totals = [part[n, block_ref[day], 0 : height[n]] for n in range(end + 1)]
         for first in range(1, N_DAY, BATCH):
             steps = range(first, min(first + BATCH, N_DAY))
             for step in steps:
-                parcel(a, step).wait_recv()
+                for n in range(end + 1):
+                    parcel(n, step).wait_recv()
             for step in steps:
-                values = slots[a, step - 1].astype(jnp.int32).astype(jnp.float32)
-                levels = jnp.where(diagonal, values[CODED : CODED + 1], 0.0)
-                level = jnp.sum(levels, axis=1, keepdims=True)
-                total = total + values * (jnp.exp2(level * (1.0 / STEPS)) * (1.0 / PEAK))
-        for group in range(G):
-            for b in range(3):
-                row = (group * 3 + b) * PB
+                values = [slots[n, step - 1] for n in range(end)] + [slots_last[step - 1]]
+                values = [v.astype(jnp.int32).astype(jnp.float32) for v in values]
+                coding = values[end][PAIR : PAIR + 1]
+                for n in range(end + 1):
+                    level = jnp.sum(jnp.where(diagonal[n], coding, 0.0), axis=1, keepdims=True)
+                    totals[n] += values[n] * (jnp.exp2(level * (1.0 / STEPS)) * (1.0 / PEAK))
+        for pair in range(9):
+            for group in range(G):
+                row = (pair % 2 * G + group) * PB
                 for r in range(PB):
-                    out_ref[r, 3 * a + b, group : group + 1, :] = total[row + r : row + r + 1]
-
-    def twice(a, tile):
+                    out_ref[r, pair, group : group + 1, :] = totals[pair // 2][row + r : row + r + 1]
+
+    def twice(pair):
         def body(block, carry):
-            unit(a, block, tile)
+            unit(pair, block)
             return carry
 
         lax.fori_loop(0, 2, body, 0)
 
-    for a in range(3):
-        for tile in range(3):
-            twice(a, tile)
-        post(a)
-    for a in range(3):
-        finish(a)
+    hand_over(0)
+    take(0)
+    hand_over(1)
+    for pair in ROUNDS[0]:
+        unit(pair, 0)
+    take(1)
+    for pair in ROUNDS[0]:
+        unit(pair, 1)
+    post(0)
+    for n in range(1, end + 1):
+        for pair in ROUNDS[n]:
+            twice(pair)
+        post(n)
+    finish()
     for copy in started:
         copy.wait_send()
 
     def settle(j, carry):
-        for a in range(3):
-            parcel(a, 1 + j).wait_send()
+        for n in range(end + 1):
+            parcel(n, 1 + j).wait_send()
         return carry
 
     lax.fori_loop(0, N_DAY - 1, settle, 0)
@@ -303,7 +333,8 @@
     rec = pltpu.VMEM((SEG + 1, 3, R, F), jnp.float32)
     src = pltpu.VMEM((SEG + 1, 6 * SB, F), jnp.float32)
     rows = pltpu.VMEM((N_STA, PIECE, 6 * SB, F), jnp.bfloat16)
-    chunk = (ROWS, LAG)
+    coded = pltpu.VMEM((len(ROUNDS) - 1, N_DAY - 1, ROWS, LAG), jnp.int16)
+    last = pltpu.VMEM((N_DAY - 1, LAST, LAG), jnp.int16)
     return pl.pallas_call(
         main_kernel,
         out_shape=jax.ShapeDtypeStruct((PB, 9, G, LAG), jnp.float32),
@@ -314,16 +345,16 @@
             rows, rows,
             pltpu.VMEM((N_STA, 2, PIECE, 6 * SB, F), jnp.bfloat16),
             rec, rec, rec, src, src, src,
-            pltpu.VMEM((N_CHUNK + 1, 3 * SB, 3, 8, F), jnp.float32),
-            pltpu.VMEM((G, SB, 3, 8, 2 * F), jnp.float32),
-            pltpu.VMEM((3, N_DAY) + chunk, jnp.float32),
-            pltpu.VMEM((3, N_DAY - 1) + chunk, jnp.int16),
-            pltpu.VMEM((3, N_DAY - 1) + chunk, jnp.int16),
+            pltpu.VMEM((N_CHUNK + 1, 3 * SB, R, F), jnp.float32),
+            pltpu.VMEM((G, SB, R, 2 * F), jnp.float32),
+            pltpu.VMEM((len(ROUNDS), N_DAY, ROWS, LAG), jnp.float32),
+            coded, coded, last, last,
+            pltpu.VMEM((N_DAY - 1, 1, LAG), jnp.float32),
             dma((2,)),
             dma((N_STA - 1,)), dma((N_STA - 1,)),
-            dma((half - 1,)), dma((half - 1,)),
-            dma((half,)), dma((half,)),
-            dma((3, N_DAY - 1)), dma((3, N_DAY - 1)),
+            dma((2, half - 1)), dma((2, half - 1)),
+            dma((2, half)), dma((2, half)),
+            dma((len(ROUNDS), N_DAY - 1)), dma((len(ROUNDS), N_DAY - 1)),
         ],
         compiler_params=pltpu.CompilerParams(
             collective_id=0, has_side_effects=True, vmem_limit_bytes=VMEM_LIMIT

time: 74.4 us -> 68.7 us (0.923)
  the two profiles are of different devices: /device:TPU:17 before, /device:TPU:1 now
where the time goes in v4:
time: 68.7 us; the launch traced here: 68.5 us
  Pallas kernels  67 us (98%)
  local copies, waits for them, and re-layouts  1.44 us (2%)
    pallas_call x1, Pallas kernels, main(): pl.pallas_call(main_kernel, out_shape=jax.ShapeDtypeStruct((PB, 9, G, LAG...  65.3 us
    pallas_call x1, Pallas kernels, plan(): pl.pallas_call(plan_kernel, out_shape=(jax.ShapeDtypeStruct((N_CHUNK * CH...  1.7 us
    unnamed x1, local copies, waits for them, and re-layouts  1.44 us

profile of v4, /device:TPU:1, one launch (start us, length us, event | category | flops | bytes accessed | tf_op | source)
XLA Modules:
  0.0 68.5 jit_solution(15544722959629192630)
XLA Ops:
  0.0 1.7 %plan.1 = (s32[72]{0:T(128)}, s32[32]{0:T(128)}, f32[2,8,128]{2,1,0:T(8,128)}) custom-call(s32[1]{0:T(128)} %bitcast.day_ref, s32[2048]{0:T(1024)} %group_ref.1, s32[32]{0:T(128)} %owner_ref.1, s32[16,128]{1,0:T(8,128)} %bitcast.8), custom_call_target="tpu_custom_call" | custom-call | tf_op jit(solution)/shard_map/plan/pallas_call | solution.py:79
  1.7 65.3 %main.1 = f32[6,9,2,128]{3,2,1,0:T(2,128)} custom-call(s32[2]{0:T(128)} %root_ref.1, s32[72]{0:T(128)} %get-tuple-element.8.order_ref, s32[32]{0:T(128)} %get-tuple-element.9.block_ref, f32[2,8,128]{2,1,0:T(8,128)} %get-tuple-element.10.scale_ref, bf16[256,256]{1,0:T(8,128)(2,1)} %constant.8.clone.table_ref, bf16[16,4,2,3,24,128]{5,4,3,2,1,0:T(8,128)(2,1)} %bitcast.6), custom_call_target="tpu_custom_call" | custom-call | tf_op jit(solution)/shard_map/main/pallas_call | solution.py:338
  67.0 1.4 %copy.7 = f32[1,6,2,9,128]{4,2,3,1,0:T(2,128)} copy(f32[1,6,2,9,128]{4,2,3,1,0:T(2,128)} %bitcast.7) | data formatting | bytes 110592

commit v5 on v4

--- a/solution.py
+++ b/solution.py
@@ -26,6 +26,13 @@
 STEPS = 256.0
 PEAK = 32767.0
 BATCH = 8
+
+
+def both_ways(count):
+    ups = range(count // 2, 0, -1)
+    return [step for up in ups for step in ((up, count - up) if 2 * up < count else (up,))]
+
+
 MESH = pl.DeviceIdType.MESH
 VMEM_LIMIT = 56 * 1024 * 1024
 
@@ -132,7 +139,7 @@
             mine[:, :, row : row + SB, :] = spec[:, :, p, comp, 0:SB, :]
     pl.semaphore_wait(barrier, N_STA + N_DAY - 2)
     scatters = []
-    for step in range(1, N_STA):
+    for step in both_ways(N_STA):
         to = lax.rem(me + step, N_STA)
         scatters.append(
             push(mine.at[to], seen.at[me], a_send.at[step - 1], a_recv.at[step - 1], {"sta": to})
@@ -154,7 +161,7 @@
     lax.fori_loop(0, N_STA, widen_rec, 0)
     for k in range(3):
         rec[k][SEG] = jnp.zeros((3, R, F), jnp.float32)
-        src[k][SEG] = jnp.zeros((6 * SB, F), jnp.float32)
+        src[k][SEG] = jnp.zeros((2, 3 * SB, F), jnp.float32)
     hist[0] = jnp.zeros((3 * SB, R, F), jnp.float32)
     for copy in scatters:
         copy.wait_recv()
@@ -171,7 +178,8 @@
         piece = picked.at[lax.rem(me + N_STA - 2 * step, N_STA), block]
         return push(piece, piece, c_send.at[block, step], c_recv.at[block, step], {"sta": partner})
 
-    spreads = [[spread(block, step) for step in range(1, half)] for block in range(2)]
+    turns = both_ways(half)
+    spreads = [[spread(block, step) for step in turns] for block in range(2)]
     hands = [[hand(block, step) for step in range(half)] for block in range(2)]
     for block in range(2):
         for copy in spreads[block]:
@@ -180,8 +188,8 @@
 
     def hand_over(block):
         hands[block][0].start()
-        for step in range(1, half):
-            spreads[block][step - 1].wait_recv()
+        for i, step in enumerate(turns):
+            spreads[block][i].wait_recv()
             hands[block][step].start()
 
     def take(block):
@@ -192,10 +200,9 @@
             for i in range(PIECE):
                 rows = picked[j, block, i].astype(jnp.float32)
                 real, imag = rows[: 3 * SB], rows[3 * SB :]
-                at = pl.ds(block * 3 * SB, 3 * SB)
-                src_re[j * PIECE + i, at] = real
-                src_im[j * PIECE + i, at] = imag
-                src_dif[j * PIECE + i, at] = real - imag
+                src_re[j * PIECE + i, block] = real
+                src_im[j * PIECE + i, block] = imag
+                src_dif[j * PIECE + i, block] = real - imag
             return carry
 
         lax.fori_loop(0, N_STA, widen_src, 0)
@@ -208,9 +215,9 @@
                 t = order_ref[chunk * CHUNK + turn]
                 held = [rec[k][t, b].reshape(3, 8, F) for k in range(3)]
                 for s in range(SB):
-                    row = pl.ds((block * 3 + a) * SB + s, 8, stride=0)
+                    row = pl.ds(a * SB + s, 8, stride=0)
                     for k in range(3):
-                        product = src[k][t, row][None] * held[k]
+                        product = src[k][t, block, row][None] * held[k]
                         sums[s * 3 + k] = sums[s * 3 + k] + product.reshape(R, F)
             for i in range(3 * SB):
                 hist[chunk + 1, i] = sums[i]
@@ -249,8 +256,8 @@
         )
 
     def post(n):
-        for first in range(1, N_DAY, BATCH):
-            steps = range(first, min(first + BATCH, N_DAY))
+        for first in range(0, N_DAY - 1, BATCH):
+            steps = both_ways(N_DAY)[first : first + BATCH]
             for step in steps:
                 rows = part[n, block_ref[lax.rem(day + step, N_DAY)], 0 : height[n]]
                 largest = jnp.max(jnp.abs(rows), axis=1, keepdims=True)
@@ -274,8 +281,8 @@
 
     def finish():
         totals = [part[n, block_ref[day], 0 : height[n]] for n in range(end + 1)]
-        for first in range(1, N_DAY, BATCH):
-            steps = range(first, min(first + BATCH, N_DAY))
+        for first in range(0, N_DAY - 1, BATCH):
+            steps = both_ways(N_DAY)[first : first + BATCH]
             for step in steps:
                 for n in range(end + 1):
                     parcel(n, step).wait_recv()
@@ -331,7 +338,7 @@
     smem = pl.BlockSpec(memory_space=pltpu.SMEM)
     dma = pltpu.SemaphoreType.DMA
     rec = pltpu.VMEM((SEG + 1, 3, R, F), jnp.float32)
-    src = pltpu.VMEM((SEG + 1, 6 * SB, F), jnp.float32)
+    src = pltpu.VMEM((SEG + 1, 2, 3 * SB, F), jnp.float32)
     rows = pltpu.VMEM((N_STA, PIECE, 6 * SB, F), jnp.bfloat16)
     coded = pltpu.VMEM((len(ROUNDS) - 1, N_DAY - 1, ROWS, LAG), jnp.int16)
     last = pltpu.VMEM((N_DAY - 1, LAST, LAG), jnp.int16)

time: 68.7 us -> 67.6 us (0.984)
  Pallas kernels: 67 us -> 65.9 us
    pallas_call x1, Pallas kernels: 65.3 us -> 64.2 us  [main(): pl.pallas_call(main_kernel, out_shape=jax.ShapeDtypeStruct((PB, 9, G, LAG...]
where the time goes in v5:
time: 67.6 us; the launch traced here: 67.3 us
  Pallas kernels  65.9 us (97%)
  local copies, waits for them, and re-layouts  1.44 us (2%)
    pallas_call x1, Pallas kernels, main(): pl.pallas_call(main_kernel, out_shape=jax.ShapeDtypeStruct((PB, 9, G, LAG...  64.2 us
    pallas_call x1, Pallas kernels, plan(): pl.pallas_call(plan_kernel, out_shape=(jax.ShapeDtypeStruct((N_CHUNK * CH...  1.7 us
    unnamed x1, local copies, waits for them, and re-layouts  1.44 us

profile of v5, /device:TPU:1, one launch (start us, length us, event | category | flops | bytes accessed | tf_op | source)
XLA Modules:
  0.0 67.3 jit_solution(17985073449758174103)
XLA Ops:
  0.0 1.7 %plan.1 = (s32[72]{0:T(128)}, s32[32]{0:T(128)}, f32[2,8,128]{2,1,0:T(8,128)}) custom-call(s32[1]{0:T(128)} %bitcast.day_ref, s32[2048]{0:T(1024)} %group_ref.1, s32[32]{0:T(128)} %owner_ref.1, s32[16,128]{1,0:T(8,128)} %bitcast.8), custom_call_target="tpu_custom_call" | custom-call | tf_op jit(solution)/shard_map/plan/pallas_call | solution.py:86
  1.7 64.2 %main.1 = f32[6,9,2,128]{3,2,1,0:T(2,128)} custom-call(s32[2]{0:T(128)} %root_ref.1, s32[72]{0:T(128)} %get-tuple-element.8.order_ref, s32[32]{0:T(128)} %get-tuple-element.9.block_ref, f32[2,8,128]{2,1,0:T(8,128)} %get-tuple-element.10.scale_ref, bf16[256,256]{1,0:T(8,128)(2,1)} %constant.8.clone.table_ref, bf16[16,4,2,3,24,128]{5,4,3,2,1,0:T(8,128)(2,1)} %bitcast.6), custom_call_target="tpu_custom_call" | custom-call | tf_op jit(solution)/shard_map/main/pallas_call | solution.py:345
  65.9 1.4 %copy.7 = f32[1,6,2,9,128]{4,2,3,1,0:T(2,128)} copy(f32[1,6,2,9,128]{4,2,3,1,0:T(2,128)} %bitcast.7) | data formatting | bytes 110592
